TPU v7x, 32 devices: a whole 2x2x4 slice. The times are simulated.
32 devices in a mesh: batch: 4 (over z), token: 8 (over y, x, core).
Axes of the slice: x: 2, y: 2, z: 4, core: 2. Of those that a mesh axis runs over, the one named last changes fastest.
Arguments:
- tokens: bfloat16 [16384, 768], P(('batch', 'token')), may hold values from -9 to 9
- slot_weight: bfloat16 [768, 1024], replicated, may hold values from -2 to 2
- expert_in: bfloat16 [128, 768, 3072], P('token', None, 'batch'), may hold values from -1.7265625 to 1.7265625
- expert_out: bfloat16 [128, 3072, 768], P('token', 'batch'), may hold values from -0.6484375 to 0.6484375
Outputs:
- mixed: bfloat16 [16384, 768], P(('batch', 'token'))
All inputs are finite; a program needn't handle non-finite values.
Results may differ from a plain program's by a relative error of at most 0.023.
Values may be sent and summed in bfloat16 or wider, within the bound.
No kernel may reach another device: no remote copies, remote signals or barrier semaphores. Data moves between devices by JAX's collectives and lax.ppermute only.
A program may use at most 128 MiB of HBM per device.

v0:
```python
import jax
import jax.numpy as jnp
from jax import lax
from jax.sharding import PartitionSpec as P


def body(tokens, slot_weight, expert_in, expert_out):
    widened = tokens.astype(jnp.float32)
    scale_row = lax.rsqrt(jnp.mean(widened * widened, axis=-1, keepdims=True) + 1e-06)
    normed = (widened * scale_row).astype(jnp.bfloat16)
    logits = jnp.dot(normed, slot_weight, preferred_element_type=jnp.float32)
    column_max = lax.pmax(jnp.max(logits, axis=0), "token")
    raised = jnp.exp(logits - column_max[None, :])
    column_sum = lax.psum(jnp.sum(raised, axis=0), "token")
    dispatch = raised.astype(jnp.bfloat16)
    partial_value = jnp.einsum("ts,td->sd", dispatch, normed, preferred_element_type=jnp.float32)
    own_count = slot_weight.shape[1] // lax.axis_size("token")
    offset = lax.axis_index("token") * own_count
    own_rows = lax.psum_scatter(
        partial_value.astype(jnp.bfloat16), "token", scatter_dimension=0, tiled=True
    ).astype(jnp.float32)
    own_total = lax.dynamic_slice_in_dim(column_sum, offset, own_count, 0)
    experts_here = expert_in.shape[0]
    slot_inputs = (own_rows / own_total[:, None]).astype(jnp.bfloat16)
    slot_inputs = slot_inputs.reshape(experts_here, own_count // experts_here, tokens.shape[1])
    hidden = jnp.einsum(
        "esd,edf->esf",
        lax.all_gather(slot_inputs, "batch", axis=1, tiled=True),
        expert_in,
        preferred_element_type=jnp.float32,
    )
    hidden = jax.nn.gelu(hidden, approximate=False).astype(jnp.bfloat16)
    terms = jnp.einsum("esf,efd->esd", hidden, expert_out, preferred_element_type=jnp.float32)
    slot_outputs = lax.psum_scatter(
        terms.astype(jnp.bfloat16), "batch", scatter_dimension=1, tiled=True
    )
    combine = jax.nn.softmax(logits, axis=1).astype(jnp.bfloat16)
    slots_each = slot_outputs.shape[1]
    block_rows = lax.all_gather(slot_outputs, "token", axis=0, tiled=True)
    number = block_rows.shape[0]
    flat_rows = block_rows.reshape(number * slots_each, block_rows.shape[2])
    mixed = jnp.dot(combine, flat_rows, preferred_element_type=jnp.float32)
    return mixed.astype(jnp.bfloat16)


def solution(mesh):
    placed = (
        P(("batch", "token"), None),
        P(),
        P("token", None, "batch"),
        P("token", "batch", None),
    )
    return jax.shard_map(
        body, mesh=mesh, in_specs=placed, out_specs=P(("batch", "token"), None), check_vma=False
    )
```

profile of v0, /device:TPU:0, one launch (start us, length us, event | category | flops | bytes accessed | tf_op | source)
XLA Modules:
  0.0 166.7 jit_solution(7911845399044545035)
XLA Ops:
  6.5 0.0 copy-start
  6.5 0.0 reduce-scatter.5.cloned.1.call-start
  6.5 1.5 fusion.3
  8.0 0.1 copy-done
  8.2 0.0 copy-start.1
  8.2 3.6 %fusion.93 = (f32[512]{0:T(512)S(1)}, f32[1024]{0:T(1024)S(1)}, f32[512,1024]{1,0:T(8,128)}) fusion(bf16[768,1024]{1,0:T(8,128)(2,1)S(1)} %copy-done, bf16[512,768]{1,0:T(8,128)(2,1)} %param.4, f32[512]{0:T(512)S(1)} %add_rsqrt_fusion), kind=kOutput, calls=%fused_computation.110 | convolution fusion | flops 807533056 | bytes 4464640 | tf_op jit(solution)/shard_map/dot_general | solution.py:11
  11.8 15.1 %pmax.7 = f32[1024]{0:T(1024)S(1)} all-reduce(f32[1024]{0:T(1024)S(1)} %get-tuple-element.8), channel_id=1, replica_groups=mesh['batch'=4,'token'=8] {'token'}, use_global_device_ids=true, to_apply=%region_4.0 | all-reduce | flops 1024 | bytes 8192 | tf_op jit(solution)/shard_map/pmax | solution.py:12
  26.9 0.0 copy-done.1
  26.9 3.9 %convolution_convert_fusion = bf16[1024,768]{1,0:T(8,128)(2,1)} fusion(f32[512,1024]{1,0:T(8,128)} %get-tuple-element.11, f32[1024]{0:T(1024)S(1)} %pmax.7, bf16[512,768]{1,0:T(8,128)(2,1)S(1)} %copy-done.1, f32[512]{0:T(512)S(1)} %add_rsqrt_fusion), kind=kOutput, calls=%fused_computation.9 | convolution fusion | flops 808321024 | bytes 4462592 | tf_op jit(solution)/shard_map/ts,td->sd/dot_general | solution.py:16
  30.8 0.0 reduce-scatter.5.cloned.1.call-update
  30.8 0.0 reduce-scatter.7.cloned.1.call-start
  30.8 2.3 %fusion = (f32[512]{0:T(512)S(1)}, f32[1024]{0:T(1024)S(1)}) fusion(f32[512,1024]{1,0:T(8,128)} %get-tuple-element.11, f32[512]{0:T(512)S(1)} %get-tuple-element.7, f32[1024]{0:T(1024)S(1)} %pmax.7), kind=kLoop, calls=%fused_computation.6 | loop fusion | flops 2095616 | bytes 2109440 | tf_op jit(solution)/shard_map/reduce_sum | solution.py:37
  33.1 11.8 %psum.7 = f32[1024]{0:T(1024)S(1)} all-reduce(f32[1024]{0:T(1024)S(1)} %get-tuple-element.6), channel_id=1, replica_groups=mesh['batch'=4,'token'=8] {'token'}, use_global_device_ids=true, to_apply=%region_7.0 | all-reduce | flops 1024 | bytes 8192 | tf_op jit(solution)/shard_map/psum | solution.py:14
  44.9 0.1 dynamic_slice.3
  45.0 23.6 %reduce-scatter.5.cloned.1.call-done = bf16[128,768]{1,0:T(8,128)(2,1)} async-done(((bf16[1024,768]{1,0:T(8,128)(2,1)}), bf16[128,768]{1,0:T(8,128)(2,1)}) %reduce-scatter.5.cloned.1.call-update) | async-done | bytes 196624 | tf_op jit(solution)/shard_map/reduce_scatter | solution.py:19
  68.7 1.0 fusion.61
  69.7 19.6 %all_gather.6 = bf16[16,32,768]{2,1,0:T(8,128)(2,1)S(1)} all-gather(bf16[16,8,768]{2,1,0:T(8,128)(2,1)S(1)} %fusion.61), channel_id=1, replica_groups=mesh['batch'=4,'token'=8] {'batch'}, dimensions={1}, use_global_device_ids=true | all-gather | bytes 983040 | tf_op jit(solution)/shard_map/all_gather | solution.py:28
  89.3 8.1 %fusion.55 = (u16[32,768]{1,0:T(8,128)(2,1)S(1)}, u16[32,768]{1,0:T(8,128)(2,1)S(1)}, f32[16,32,768]{2,1,0:T(8,128)S(1)}) fusion(bf16[16,32,768]{2,1,0:T(8,128)(2,1)S(1)} %all_gather.6, bf16[16,768,768]{2,1,0:T(8,128)(2,1)} %param.6), kind=kOutput, calls=%fused_computation.71 | convolution fusion | flops 609042432 | bytes 21331968 | tf_op jit(solution)/shard_map/esd,edf->esf/dot_general | solution.py:26
  97.4 9.0 %fusion.94 = bf16[4,8,16,768]{3,1,0,2:T(8,128)(2,1)S(1)} fusion(bf16[16,768,768]{2,1,0:T(8,128)(2,1)} %param.7, f32[16,32,768]{2,1,0:T(8,128)S(1)} %get-tuple-element.12, u16[32,768]{1,0:T(8,128)(2,1)S(1)} %get-tuple-element.10, u16[32,768]{1,0:T(8,128)(2,1)S(1)} %get-tuple-element.9), kind=kOutput, calls=%fused_computation.111 | convolution fusion | flops 631898112 | bytes 21331968 | tf_op jit(solution)/shard_map/esf,efd->esd/dot_general | solution.py:33
  106.5 0.9 copy.7
  107.4 0.0 reduce-scatter.7.cloned.1.call-update
  107.4 0.0 all-gather.2.cloned.1.call-start
  107.5 21.8 %reduce-scatter.7.cloned.1.call-done = bf16[8,12288]{1,0:T(8,128)(2,1)} async-done(((bf16[32,12288]{1,0:T(8,128)(2,1)}), bf16[8,12288]{1,0:T(8,128)(2,1)}) %reduce-scatter.7.cloned.1.call-update) | async-done | bytes 196624
  129.2 1.0 copy.11
  130.2 0.7 copy.6
  130.9 0.0 all-gather.2.cloned.1.call-update
  131.0 25.3 %all-gather.2.cloned.1.call-done = bf16[128,8,768]{2,1,0:T(8,128)(2,1)} async-done(((bf16[16,8,768]{2,1,0:T(8,128)(2,1)}), bf16[128,8,768]{2,1,0:T(8,128)(2,1)}) %all-gather.2.cloned.1.call-update) | async-done | bytes 1572880 | tf_op jit(solution)/shard_map/all_gather | solution.py:39
  156.2 4.0 %fusion.16 = bf16[512,768]{1,0:T(8,128)(2,1)} fusion(bf16[128,8,768]{2,1,0:T(8,128)(2,1)} %all-gather.2.cloned.1.call-done, f32[512,1024]{1,0:T(8,128)} %get-tuple-element.11, f32[512]{0:T(512)S(1)} %get-tuple-element.5, f32[512]{0:T(512)S(1)} %get-tuple-element.7), kind=kOutput, calls=%fused_computation.35 | convolution fusion | flops 807272448 | bytes 4460544 | tf_op jit(solution)/shard_map/dot_general | solution.py:42
  (1 shorter events, 0.0 us)
Async XLA Ops:
  6.5 1.6 copy-start
  6.5 62.1 %reduce-scatter.5.cloned.1.call-start = ((), (), s32[]{:S(2)}) async-start(), calls=%async_computation.2 | async-start | bytes 1769472 | tf_op jit(solution)/shard_map/reduce_scatter | solution.py:19
  8.2 18.7 %copy-start.1 = (bf16[512,768]{1,0:T(8,128)(2,1)S(1)}, bf16[512,768]{1,0:T(8,128)(2,1)}, u32[]{:S(2)}) copy-start(bf16[512,768]{1,0:T(8,128)(2,1)} %param.4) | copy-start | bytes 2359300
  30.8 98.4 %reduce-scatter.7.cloned.1.call-start = ((), (), s32[]{:S(2)}) async-start(), calls=%async_computation.4 | async-start | bytes 983040
  107.4 48.8 %all-gather.2.cloned.1.call-start = ((), (), s32[]{:S(2)}) async-start(), calls=%async_computation.3 | async-start | bytes 1769472 | tf_op jit(solution)/shard_map/all_gather | solution.py:39
Sparse Core Ops, SparseCore 0:
  30.9 37.7 reduce-scatter.4
  107.5 21.6 reduce-scatter.6
  131.1 25.0 all-gather.1
where the time goes:
time: 167 us
  waiting for transfers between devices  70.7 us (42%)
  blocking collectives  46.5 us (28%)
  matrix products  28.6 us (17%)
  between operations  13.1 us (8%)
  other arithmetic  4.83 us (3%)
  local copies, waits for them, and re-layouts  2.86 us (2%)
    all_gather x1, waiting for transfers between devices, body(): block_rows = lax.all_gather(slot_outputs, 'token', axis=0, tiled=True)  25.3 us
    reduce_scatter x1, waiting for transfers between devices, body(): lax.psum_scatter(partial_value.astype(jnp.bfloat16), 'token', scatter_dim...  23.6 us
    unnamed x4, waiting for transfers between devices  21.8 us
    all_gather x1, blocking collectives, body(): lax.all_gather(slot_inputs, 'batch', axis=1, tiled=True)  19.6 us
    pmax x1, blocking collectives, body(): column_max = lax.pmax(jnp.max(logits, axis=0), 'token')  15.1 us
    psum x1, blocking collectives, body(): column_sum = lax.psum(jnp.sum(raised, axis=0), 'token')  11.8 us
    dot_general x1, matrix products, body(): jnp.einsum('esf,efd->esd', hidden, expert_out, preferred_element_type=jnp...  9.04 us
    dot_general x1, matrix products, body(): jnp.einsum('esd,edf->esf', lax.all_gather(slot_inputs, 'batch', axis=1, t...  8.12 us
  transfers between devices with their start and end apart: 3, of which 3 were waited for; matrix products, arithmetic and copies ran while one was open for 1% of the time, Pallas kernels for 0%

commit v1 on v0

--- a/solution.py
+++ b/solution.py
@@ -1,7 +1,41 @@
+import functools
 import jax
 import jax.numpy as jnp
 from jax import lax
 from jax.sharding import PartitionSpec as P
+
+
+def prepare_strings(array_in, array_axis):
+    array_in = jnp.moveaxis(array_in, 0, array_axis)
+    piece_next = array_in.shape
+    local_out = array_in.reshape(
+        *piece_next[:array_axis],
+        piece_next[array_axis] * piece_next[array_axis + 1],
+        *piece_next[array_axis + 2 :]
+    )
+    return local_out
+
+
+def plan_the_spots(in_array, dev_axis):
+    v_next = in_array[None]
+    world_n = lax.axis_size(dev_axis)
+    for c in range(world_n.bit_length() - 1):
+        state_next = 1 << c
+        reply = lax.ppermute(
+            v_next, axis_name=dev_axis, perm=[(s, s ^ state_next) for s in range(world_n)]
+        )
+        val = jnp.stack([v_next, reply])
+        front = lax.axis_index(dev_axis) >> c & 1
+        v_next = jnp.where(front == 0, val, val[::-1]).reshape(-1, *in_array.shape)
+    return v_next
+
+
+def lift_the_widths(vec, point, in_dim):
+    block_now = prepare_strings(plan_the_spots(vec, point), in_dim)
+    return block_now
+
+
+unite_frame = functools.partial(lift_the_widths, point="token", in_dim=0)
 
 
 def body(tokens, slot_weight, expert_in, expert_out):
@@ -36,7 +70,7 @@
     )
     combine = jax.nn.softmax(logits, axis=1).astype(jnp.bfloat16)
     slots_each = slot_outputs.shape[1]
-    block_rows = lax.all_gather(slot_outputs, "token", axis=0, tiled=True)
+    block_rows = unite_frame(slot_outputs)
     number = block_rows.shape[0]
     flat_rows = block_rows.reshape(number * slots_each, block_rows.shape[2])
     mixed = jnp.dot(combine, flat_rows, preferred_element_type=jnp.float32)

time: 167 us -> 173 us (1.036)
  starting transfers between devices: 0.09 us -> 3.19 us
  waiting for transfers between devices: 70.7 us -> 73.8 us
  matrix products: 28.6 us -> 26.5 us
    ppermute x0 -> x3, waiting for transfers between devices: none -> 28.4 us  [plan_the_spots(): lax.ppermute(v_next, axis_name=dev_axis, perm=[(s, s ^ state_next) for s...]
    all_gather x1 -> x0, waiting for transfers between devices: 25.3 us -> none  [body(): block_rows = lax.all_gather(slot_outputs, 'token', axis=0, tiled=True)]
    ppermute x0 -> x3, starting transfers between devices: none -> 3.14 us  [plan_the_spots(): lax.ppermute(v_next, axis_name=dev_axis, perm=[(s, s ^ state_next) for s...]
    dot_general x1, matrix products: 4 us -> 1.96 us  [body(): mixed = jnp.dot(combine, flat_rows, preferred_element_type=jnp.float32)]
    unnamed x4 -> x3, waiting for transfers between devices: 21.8 us -> 21.8 us
  transfers between devices with their start and end apart: 3 -> 5, of which waited for: 3 -> 5; matrix products, arithmetic and copies ran while one was open for 1% -> 1% of each run, Pallas kernels for 0% -> 0%
where the time goes in v1:
time: 173 us
  waiting for transfers between devices  73.8 us (43%)
  blocking collectives  46.5 us (27%)
  matrix products  26.5 us (15%)
  between operations  13.5 us (8%)
  other arithmetic  5.58 us (3%)
  local copies, waits for them, and re-layouts  3.49 us (2%)
  starting transfers between devices  3.19 us (2%)
    ppermute x3, waiting for transfers between devices, plan_the_spots(): lax.ppermute(v_next, axis_name=dev_axis, perm=[(s, s ^ state_next) for s...  28.4 us
    reduce_scatter x1, waiting for transfers between devices, body(): lax.psum_scatter(partial_value.astype(jnp.bfloat16), 'token', scatter_dim...  23.6 us
    unnamed x3, waiting for transfers between devices  21.8 us
    all_gather x1, blocking collectives, body(): lax.all_gather(slot_inputs, 'batch', axis=1, tiled=True)  19.6 us
    pmax x1, blocking collectives, body(): column_max = lax.pmax(jnp.max(logits, axis=0), 'token')  15.1 us
    psum x1, blocking collectives, body(): column_sum = lax.psum(jnp.sum(raised, axis=0), 'token')  11.8 us
    dot_general x1, matrix products, body(): jnp.einsum('esf,efd->esd', hidden, expert_out, preferred_element_type=jnp...  9.03 us
    dot_general x1, matrix products, body(): jnp.einsum('esd,edf->esf', lax.all_gather(slot_inputs, 'batch', axis=1, t...  8.12 us
  transfers between devices with their start and end apart: 5, of which 5 were waited for; matrix products, arithmetic and copies ran while one was open for 1% of the time, Pallas kernels for 0%

profile of v1, /device:TPU:0, one launch (start us, length us, event | category | flops | bytes accessed | tf_op | source)
XLA Modules:
  0.0 172.7 jit_solution(16960355442225360237)
XLA Ops:
  6.5 0.0 copy-start
  6.5 0.0 reduce-scatter.5.cloned.1.call-start
  6.5 1.5 fusion.3
  8.0 0.1 copy-done
  8.2 0.0 copy-start.2
  8.2 3.6 %fusion.90 = (f32[512]{0:T(512)S(1)}, f32[1024]{0:T(1024)S(1)}, f32[512,1024]{1,0:T(8,128)}) fusion(bf16[768,1024]{1,0:T(8,128)(2,1)S(1)} %copy-done, bf16[512,768]{1,0:T(8,128)(2,1)} %param.4, f32[512]{0:T(512)S(1)} %add_rsqrt_fusion), kind=kOutput, calls=%fused_computation.118 | convolution fusion | flops 807533056 | bytes 4464640 | tf_op jit(solution)/shard_map/dot_general | solution.py:45
  11.8 15.1 %pmax.7 = f32[1024]{0:T(1024)S(1)} all-reduce(f32[1024]{0:T(1024)S(1)} %get-tuple-element.8), channel_id=1, replica_groups=mesh['batch'=4,'token'=8] {'token'}, use_global_device_ids=true, to_apply=%region_4.0 | all-reduce | flops 1024 | bytes 8192 | tf_op jit(solution)/shard_map/pmax | solution.py:46
  26.9 0.0 copy-done.2
  26.9 3.9 %convolution_convert_fusion = bf16[1024,768]{1,0:T(8,128)(2,1)} fusion(f32[512,1024]{1,0:T(8,128)} %get-tuple-element.15, f32[1024]{0:T(1024)S(1)} %pmax.7, bf16[512,768]{1,0:T(8,128)(2,1)S(1)} %copy-done.2, f32[512]{0:T(512)S(1)} %add_rsqrt_fusion), kind=kOutput, calls=%fused_computation.10 | convolution fusion | flops 808321024 | bytes 4462592 | tf_op jit(solution)/shard_map/ts,td->sd/dot_general | solution.py:50
  30.8 0.0 reduce-scatter.5.cloned.1.call-update
  30.8 0.0 reduce-scatter.7.cloned.1.call-start
  30.8 2.3 %fusion = (f32[512]{0:T(512)S(1)}, f32[1024]{0:T(1024)S(1)}) fusion(f32[512,1024]{1,0:T(8,128)} %get-tuple-element.15, f32[512]{0:T(512)S(1)} %get-tuple-element.7, f32[1024]{0:T(1024)S(1)} %pmax.7), kind=kLoop, calls=%fused_computation.7 | loop fusion | flops 2095616 | bytes 2109440 | tf_op jit(solution)/shard_map/reduce_sum | solution.py:71
  33.1 11.8 %psum.7 = f32[1024]{0:T(1024)S(1)} all-reduce(f32[1024]{0:T(1024)S(1)} %get-tuple-element.6), channel_id=1, replica_groups=mesh['batch'=4,'token'=8] {'token'}, use_global_device_ids=true, to_apply=%region_7.0 | all-reduce | flops 1024 | bytes 8192 | tf_op jit(solution)/shard_map/psum | solution.py:48
  44.9 0.1 dynamic_slice.3
  45.0 23.6 %reduce-scatter.5.cloned.1.call-done = bf16[128,768]{1,0:T(8,128)(2,1)} async-done(((bf16[1024,768]{1,0:T(8,128)(2,1)}), bf16[128,768]{1,0:T(8,128)(2,1)}) %reduce-scatter.5.cloned.1.call-update) | async-done | bytes 196624 | tf_op jit(solution)/shard_map/reduce_scatter | solution.py:53
  68.7 1.0 fusion.58
  69.7 19.6 %all_gather.3 = bf16[16,32,768]{2,1,0:T(8,128)(2,1)S(1)} all-gather(bf16[16,8,768]{2,1,0:T(8,128)(2,1)S(1)} %fusion.58), channel_id=1, replica_groups=mesh['batch'=4,'token'=8] {'batch'}, dimensions={1}, use_global_device_ids=true | all-gather | bytes 983040 | tf_op jit(solution)/shard_map/all_gather | solution.py:62
  89.3 8.1 %fusion.50 = (u16[32,768]{1,0:T(8,128)(2,1)S(1)}, u16[32,768]{1,0:T(8,128)(2,1)S(1)}, f32[16,32,768]{2,1,0:T(8,128)S(1)}) fusion(bf16[16,32,768]{2,1,0:T(8,128)(2,1)S(1)} %all_gather.3, bf16[16,768,768]{2,1,0:T(8,128)(2,1)} %param.6), kind=kOutput, calls=%fused_computation.73 | convolution fusion | flops 609042432 | bytes 21331968 | tf_op jit(solution)/shard_map/esd,edf->esf/dot_general | solution.py:60
  97.4 9.0 %fusion.91 = bf16[4,8,16,768]{3,1,0,2:T(8,128)(2,1)S(1)} fusion(bf16[16,768,768]{2,1,0:T(8,128)(2,1)} %param.7, f32[16,32,768]{2,1,0:T(8,128)S(1)} %get-tuple-element.16, u16[32,768]{1,0:T(8,128)(2,1)S(1)} %get-tuple-element.10, u16[32,768]{1,0:T(8,128)(2,1)S(1)} %get-tuple-element.9), kind=kOutput, calls=%fused_computation.119 | convolution fusion | flops 631898112 | bytes 21331968 | tf_op jit(solution)/shard_map/esf,efd->esd/dot_general | solution.py:67
  106.4 0.9 copy.7
  107.4 0.0 reduce-scatter.7.cloned.1.call-update
  107.4 21.8 %reduce-scatter.7.cloned.1.call-done = bf16[8,12288]{1,0:T(8,128)(2,1)} async-done(((bf16[32,12288]{1,0:T(8,128)(2,1)}), bf16[8,12288]{1,0:T(8,128)(2,1)}) %reduce-scatter.7.cloned.1.call-update) | async-done | bytes 196624
  129.2 1.0 copy.13
  130.2 0.1 copy.14
  130.2 0.1 collective-permute-start
  130.3 1.4 collective-permute-done
  131.8 0.1 fusion.57
  131.9 1.5 collective-permute-start.1
  133.4 9.7 %collective-permute-done.1 = bf16[2,16,8,768]{3,2,1,0:T(8,128)(2,1)S(1)} collective-permute-done((bf16[2,16,8,768]{3,2,1,0:T(8,128)(2,1)S(1)}, bf16[2,16,8,768]{3,2,1,0:T(8,128)(2,1)S(1)}, u32[]{:S(2)}, u32[]{:S(2)}) %collective-permute-start.1) | collective-permute-done | bytes 393248 | tf_op jit(solution)/shard_map/ppermute | solution.py:24
  143.1 0.1 pad_maximum_fusion.1
  143.2 0.1 reverse_select_fusion.1
  143.3 1.5 collective-permute-start.2
  144.9 17.2 %collective-permute-done.2 = bf16[4,16,8,768]{3,2,1,0:T(8,128)(2,1)S(1)} collective-permute-done((bf16[4,16,8,768]{3,2,1,0:T(8,128)(2,1)S(1)}, bf16[4,16,8,768]{3,2,1,0:T(8,128)(2,1)S(1)}, u32[]{:S(2)}, u32[]{:S(2)}) %collective-permute-start.2) | collective-permute-done | bytes 786464 | tf_op jit(solution)/shard_map/ppermute | solution.py:24
  162.1 0.1 pad_maximum_fusion
  162.3 0.0 copy-start.1
  162.3 0.3 reverse_select_fusion
  162.5 1.3 copy-done.1
  163.9 2.0 %convolution_convert_fusion.1 = bf16[512,768]{1,0:T(8,128)(2,1)} fusion(bf16[1024,768]{1,0:T(8,128)(2,1)S(1)} %bitcast.37, f32[512,1024]{1,0:T(8,128)S(1)} %copy-done.1, f32[512]{0:T(512)S(1)} %get-tuple-element.5, f32[512]{0:T(512)S(1)} %get-tuple-element.7), kind=kOutput, calls=%fused_computation.35 | convolution fusion | flops 807272448 | bytes 4460544 | tf_op jit(solution)/shard_map/dot_general | solution.py:76
  (2 shorter events, 0.0 us)
Async XLA Ops:
  6.5 1.6 copy-start
  6.5 62.1 %reduce-scatter.5.cloned.1.call-start = ((), (), s32[]{:S(2)}) async-start(), calls=%async_computation.2 | async-start | bytes 1769472 | tf_op jit(solution)/shard_map/reduce_scatter | solution.py:53
  8.2 18.7 %copy-start.2 = (bf16[512,768]{1,0:T(8,128)(2,1)S(1)}, bf16[512,768]{1,0:T(8,128)(2,1)}, u32[]{:S(2)}) copy-start(bf16[512,768]{1,0:T(8,128)(2,1)} %param.4) | copy-start | bytes 2359300
  30.8 98.4 %reduce-scatter.7.cloned.1.call-start = ((), (), s32[]{:S(2)}) async-start(), calls=%async_computation.3 | async-start | bytes 983040
  130.2 1.5 collective-permute-start
  131.9 11.2 %collective-permute-start.1 = (bf16[2,16,8,768]{3,2,1,0:T(8,128)(2,1)S(1)}, bf16[2,16,8,768]{3,2,1,0:T(8,128)(2,1)S(1)}, u32[]{:S(2)}, u32[]{:S(2)}) collective-permute-start(bf16[2,16,8,768]{3,2,1,0:T(8,128)(2,1)S(1)} %get-tuple-element.12), channel_id=1, source_target_pairs={{0,2},{1,3},{2,0},{3,1},{4,6},{5,7},{6,4},{7,5},{8,10},{9,11},{10,... | collective-permute-start | bytes 1179656 | tf_op jit(solution)/shard_map/ppermute | solution.py:24
  143.3 18.8 %collective-permute-start.2 = (bf16[4,16,8,768]{3,2,1,0:T(8,128)(2,1)S(1)}, bf16[4,16,8,768]{3,2,1,0:T(8,128)(2,1)S(1)}, u32[]{:S(2)}, u32[]{:S(2)}) collective-permute-start(bf16[4,16,8,768]{3,2,1,0:T(8,128)(2,1)S(1)} %bitcast.35), channel_id=1, source_target_pairs={{0,4},{1,5},{2,6},{3,7},{4,0},{5,1},{6,2},{7,3},{8,12},{9,13},{10,... | collective-permute-start | bytes 2359304 | tf_op jit(solution)/shard_map/ppermute | solution.py:24
  162.3 1.6 copy-start.1
Sparse Core Ops, SparseCore 0:
  30.9 37.7 reduce-scatter.4
  107.5 21.6 reduce-scatter.6
